TPU v7x, 256 devices: a whole 4x4x8 slice. The times are simulated.
256 devices in a mesh: pair: 64 (over y, z, core), batch: 4 (over x).
Axes of the slice: x: 4, y: 4, z: 8, core: 2. Of those that a mesh axis runs over, the one named last changes fastest.
Arguments:
- ao_ints: bfloat16 [32768, 4096], P('pair', 'batch'), may hold values from -6 to 6
- shell_mask: int32 [512, 64], P('pair', 'batch'), may hold values 0 or 1
- bra_shells: int32 [512, 2], replicated, may hold values from 0 to 749
- ket_shells: int32 [64, 2], P('batch'), may hold values from 0 to 749
- mo_coeff: bfloat16 [6000, 256], replicated, may hold values from -0.59765625 to 0.59765625
- mo_ranges: int32 [4], replicated, may hold values from 0 to 192
Outputs:
- transformed: float32 [4096, 1024], P(('pair', 'batch'))
All inputs are finite; a program needn't handle non-finite values. No bound on the sum of `shell_mask` on one device may be relied on, other than what follows from the above.
Results may differ from a plain program's by a relative error of at most 0.0049.
Values may be sent and summed in bfloat16 or wider, within the bound.
A program may use at most 64 MiB of HBM per device.

v0:
```python
import math

import jax
import jax.numpy as jnp
from jax import lax
from jax.sharding import PartitionSpec as P

SHELL = 8
NI = 64
NA = 32


def window_cols(mo_coeff, start, count):
    picked = lax.dynamic_slice_in_dim(mo_coeff, start, count, 1)
    return picked.reshape(mo_coeff.shape[0] // SHELL, SHELL, count)


def lookup_rows(table, shell_ids):
    shell_total = table.shape[0]
    flat_table = table.reshape(shell_total, SHELL * table.shape[2])
    choose = (
        shell_ids[:, None] == lax.broadcasted_iota(jnp.int32, (shell_ids.shape[0], shell_total), 1)
    ).astype(jnp.bfloat16)
    picked = jnp.dot(choose, flat_table, preferred_element_type=jnp.float32)
    return picked.astype(jnp.bfloat16).reshape(shell_ids.shape[0] * SHELL, table.shape[2])


def outer_rows(first_cols, second_cols, shells):
    count_one = first_cols.shape[2]
    count_two = second_cols.shape[2]
    width = count_one * count_two
    rows_one = lookup_rows(first_cols, shells[:, 0])
    rows_two = lookup_rows(second_cols, shells[:, 1])
    column_ids = lax.broadcasted_iota(jnp.int32, (count_one, width), 1)
    repeat_table = (
        column_ids // count_two == lax.broadcasted_iota(jnp.int32, (count_one, width), 0)
    ).astype(jnp.bfloat16)
    column_two = lax.broadcasted_iota(jnp.int32, (count_two, width), 1)
    tile_table = (
        column_two % count_two == lax.broadcasted_iota(jnp.int32, (count_two, width), 0)
    ).astype(jnp.bfloat16)
    spread_one = jnp.dot(rows_one, repeat_table, preferred_element_type=jnp.float32)
    spread_two = jnp.dot(rows_two, tile_table, preferred_element_type=jnp.float32)
    shell_count = shells.shape[0]
    product = spread_one.reshape(shell_count, SHELL, 1, width) * spread_two.reshape(
        shell_count, 1, SHELL, width
    )
    return product.reshape(shell_count * SHELL * SHELL, width).astype(jnp.bfloat16)


def bra_contract(flattened, bra_shells, first_cols, second_cols):
    shell_count = bra_shells.shape[0]
    group_size = math.gcd(shell_count, 32)
    block_rows = group_size * SHELL * SHELL
    starting = jnp.zeros(
        (flattened.shape[0], first_cols.shape[2] * second_cols.shape[2]), jnp.float32
    )

    def advance(running_sum, group_index):
        shells = lax.dynamic_slice_in_dim(bra_shells, group_index * group_size, group_size, 0)
        coeff_block = outer_rows(first_cols, second_cols, shells)
        upper_block = lax.dynamic_slice_in_dim(flattened, group_index * block_rows, block_rows, 1)
        contribution = jnp.dot(upper_block, coeff_block, preferred_element_type=jnp.float32)
        return (running_sum + contribution, None)

    result, unused = lax.scan(
        advance, starting, jnp.arange(shell_count // group_size, dtype=jnp.int32)
    )
    return result


def on_device(ao_ints, shell_mask, bra_shells, ket_shells, mo_coeff, mo_ranges):
    ket_coeff = outer_rows(
        window_cols(mo_coeff, mo_ranges[0], NI), window_cols(mo_coeff, mo_ranges[1], NI), ket_shells
    )
    bra_first = window_cols(mo_coeff, mo_ranges[2], NA)
    bra_second = window_cols(mo_coeff, mo_ranges[3], NA)
    local_bra = shell_mask.shape[0]
    local_ket = shell_mask.shape[1]
    block_mask = shell_mask.astype(jnp.bfloat16)
    screened = (
        ao_ints.reshape(local_bra, SHELL * SHELL, local_ket, SHELL * SHELL)
        * block_mask[:, None, :, None]
    ).reshape(ao_ints.shape)
    halfway = lax.dot_general(
        ket_coeff, screened, (((0,), (1,)), ((), ())), preferred_element_type=jnp.float32
    ).astype(jnp.bfloat16)
    pair_count = lax.axis_size("pair")
    bra_rows = ao_ints.shape[0]
    outgoing = halfway.reshape(pair_count, -1, bra_rows)
    received = lax.all_to_all(outgoing, "pair", split_axis=0, concat_axis=2, tiled=True)
    flattened = received.reshape(received.shape[1], received.shape[2])
    partial_value = bra_contract(flattened, bra_shells, bra_first, bra_second)
    return lax.psum_scatter(partial_value, "batch", scatter_dimension=0, tiled=True)


def solution(mesh):
    return jax.shard_map(
        on_device,
        mesh=mesh,
        in_specs=(P("pair", "batch"), P("pair", "batch"), P(), P("batch", None), P(), P()),
        out_specs=P(("pair", "batch"), None),
        check_vma=False,
    )
```

profile of v0, /device:TPU:1, one launch (start us, length us, event | category | flops | bytes accessed | tf_op | source)
XLA Modules:
  0.0 343.2 jit_solution(16499854220420385860)
XLA Ops:
  6.5 1.5 fusion.43
  11.9 3.9 %constant_dynamic-slice_fusion.4 = (bf16[6000,64]{1,0:T(8,128)(2,1)S(1)}, bf16[6000,64]{1,0:T(8,128)(2,1)S(1)}) fusion(bf16[6000,256]{1,0:T(8,128)(2,1)} %param.12, s32[]{:T(128)S(6)} %select_n.55, s32[]{:T(128)S(6)} %select_n.57), kind=kLoop, calls=%fused_computation.69 | loop fusion | bytes 3072008 | tf_op jit(solution)/shard_map/dynamic_slice | solution.py:14
  15.9 2.0 reshape_reshape.18
  17.9 1.4 convolution_convert_fusion.4
  21.2 1.5 mul.66
  23.1 1.8 fusion.27
  24.9 6.7 %multiply_convert_fusion.1 = bf16[16,8,8,4096]{3,2,1,0:T(8,128)(2,1)} fusion(f32[16,8,4096]{2,1,0:T(8,128)} %fusion.27, f32[16,8,4096]{2,1,0:T(8,128)S(1)} %fusion.24), kind=kLoop, calls=%fused_computation.35 | loop fusion | flops 8388608 | bytes 12582912 | tf_op jit(solution)/shard_map/convert_element_type | solution.py:48
  31.6 10.2 %convolution_convert_fusion.2 = bf16[4096,512]{1,0:T(8,128)(2,1)} fusion(bf16[1024,4096]{1,0:T(8,128)(2,1)} %bitcast.83, bf16[512,1024]{1,0:T(8,128)(2,1)} %param.8, bf16[512,1024]{1,0:T(8,128)(2,1)S(1)} %mul.66), kind=kOutput, calls=%fused_computation.36 | convolution fusion | flops 4297588736 | bytes 14680064 | tf_op jit(solution)/shard_map/dot_general | solution.py:85
  41.8 13.7 %all-to-all-start = ((bf16[64,64,512]{2,1,0:T(8,128)(2,1)}), bf16[64,64,512]{2,1,0:T(8,128)(2,1)}, u32[]{:S(2)}, u32[]{:S(2)}) async-start(bf16[64,64,512]{2,1,0:T(8,128)(2,1)} %bitcast.85), calls=%async_computation | async-start | bytes 8388608 | tf_op jit(solution)/shard_map/all_to_all | solution.py:91
  59.5 2.7 constant_dynamic-slice_fusion.1
  62.2 2.3 reshape_reshape.22
  64.6 2.3 reshape_reshape.23
  66.9 84.5 %all-to-all-done = bf16[64,64,512]{2,1,0:T(8,128)(2,1)} async-done(((bf16[64,64,512]{2,1,0:T(8,128)(2,1)}), bf16[64,64,512]{2,1,0:T(8,128)(2,1)}, u32[]{:S(2)}, u32[]{:S(2)}) %all-to-all-start) | async-done | bytes 4194336 | tf_op jit(solution)/shard_map/all_to_all | solution.py:91
  151.4 4.6 %copy.9 = bf16[8,8,64,512]{3,1,2,0:T(8,128)(2,1)} copy(bf16[8,8,64,512]{3,1,0,2:T(8,128)(2,1)} %bitcast.36) | data formatting | bytes 8388608
  155.9 162.2 %while.14 = (s32[]{:T(128)}, f32[64,1024]{1,0:T(8,128)S(1)}, s32[16]{0:T(128)S(1)}, bf16[64,32768]{1,0:T(8,128)(2,1)}, s32[512,2]{0,1:T(2,128)}, /*index=5*/bf16...) while((s32[]{:T(128)}, f32[64,1024]{1,0:T(8,128)S(1)}, ...), condition=%wide.wide.region_1.2_spmd.clone, body=%wide.wide.region_0.1_spmd.clone.sunk | while | flops 331100032 | bytes 14306823 | solution.py:66
  159.2 3.1 multiply_convert_fusion.4
  162.9 3.2 convolution_add_fusion.3
  169.3 3.1 multiply_convert_fusion.4
  173.0 3.2 convolution_add_fusion.3
  179.5 3.1 multiply_convert_fusion.4
  183.2 3.2 convolution_add_fusion.3
  189.6 3.1 multiply_convert_fusion.4
  193.3 3.2 convolution_add_fusion.3
  199.7 3.1 multiply_convert_fusion.4
  203.5 3.2 convolution_add_fusion.3
  209.9 3.1 multiply_convert_fusion.4
  213.6 3.2 convolution_add_fusion.3
  220.0 3.1 multiply_convert_fusion.4
  223.7 3.2 convolution_add_fusion.3
  230.2 3.1 multiply_convert_fusion.4
  233.9 3.2 convolution_add_fusion.3
  240.3 3.1 multiply_convert_fusion.4
  244.0 3.2 convolution_add_fusion.3
  250.4 3.1 multiply_convert_fusion.4
  254.1 3.2 convolution_add_fusion.3
  260.6 3.1 multiply_convert_fusion.4
  264.3 3.2 convolution_add_fusion.3
  270.7 3.1 multiply_convert_fusion.4
  274.4 3.2 convolution_add_fusion.3
  280.8 3.1 multiply_convert_fusion.4
  284.6 3.2 convolution_add_fusion.3
  291.0 3.1 multiply_convert_fusion.4
  294.7 3.2 convolution_add_fusion.3
  301.1 3.1 multiply_convert_fusion.4
  304.8 3.2 convolution_add_fusion.3
  311.3 3.1 multiply_convert_fusion.4
  315.0 3.2 convolution_add_fusion.3
  318.9 17.5 %reduce-scatter.2.cloned.1.call-done = f32[16,1024]{1,0:T(8,128)} async-done(((f32[64,1024]{1,0:T(8,128)}), f32[16,1024]{1,0:T(8,128)}) %reduce-scatter.2.cloned.1.call-update) | async-done | bytes 65552 | tf_op jit(solution)/shard_map/reduce_scatter | solution.py:94
  (232 shorter events, 44.3 us)
Async XLA Ops:
  11.9 6.0 %copy-start.3 = (s32[16,2]{0,1:T(2,128)S(1)}, s32[16,2]{0,1:T(2,128)}, u32[]{:S(2)}) copy-start(s32[16,2]{0,1:T(2,128)} %param.11) | copy-start | bytes 388
  15.9 5.0 %copy-start.2 = (s32[8,16]{1,0:T(8,128)S(1)}, s32[8,16]{1,0:T(8,128)}, u32[]{:S(2)}) copy-start(s32[8,16]{1,0:T(8,128)} %param.9) | copy-start | bytes 1540
  41.8 17.7 %copy-start = (bf16[6000,256]{1,0:T(8,128)(2,1)S(1)}, bf16[6000,256]{1,0:T(8,128)(2,1)}, u32[]{:S(2)}) copy-start(bf16[6000,256]{1,0:T(8,128)(2,1)} %param.12) | copy-start | bytes 9216004
  41.8 109.5 %all-to-all-start = ((bf16[64,64,512]{2,1,0:T(8,128)(2,1)}), bf16[64,64,512]{2,1,0:T(8,128)(2,1)}, u32[]{:S(2)}, u32[]{:S(2)}) async-start(bf16[64,64,512]{2,1,0:T(8,128)(2,1)} %bitcast.85), calls=%async_computation | async-start | bytes 8388608 | tf_op jit(solution)/shard_map/all_to_all | solution.py:91
  55.5 280.9 %reduce-scatter.2.cloned.1.call-start = ((), (), s32[]{:S(2)}) async-start(), calls=%async_computation.2 | async-start | bytes 327680 | tf_op jit(solution)/shard_map/reduce_scatter | solution.py:94
  318.2 0.7 copy-start.1
Sparse Core Ops, SparseCore 0:
  319.0 17.3 reduce-scatter.1
where the time goes:
time: 346 us; the launch traced here: 343 us
  waiting for transfers between devices  102 us (29%)
  matrix products  80.3 us (23%)
  other arithmetic  57.3 us (17%)
  local copies, waits for them, and re-layouts  48.7 us (14%)
  between operations  21.4 us (6%)
  loops' own time  20 us (6%)
  starting transfers between devices  13.7 us (4%)
    all_to_all x1, waiting for transfers between devices, on_device(): lax.all_to_all(outgoing, 'pair', split_axis=0, concat_axis=2, tiled=True)  84.5 us
    convert_element_type x17, other arithmetic, outer_rows(): product.reshape(shell_count * SHELL * SHELL, width).astype(jnp.bfloat16)  56.9 us
    dot_general x16, matrix products, advance(): jnp.dot(upper_block, coeff_block, preferred_element_type=jnp.float32)  50.9 us
    another operation x1, loops' own time, bra_contract(): lax.scan(advance, starting, jnp.arange(shell_count // group_size, dtype=j...  20 us
    reduce_scatter x1, waiting for transfers between devices, on_device(): lax.psum_scatter(partial_value, 'batch', scatter_dimension=0, tiled=True)  17.5 us
    all_to_all x1, starting transfers between devices, on_device(): lax.all_to_all(outgoing, 'pair', split_axis=0, concat_axis=2, tiled=True)  13.7 us
    dynamic_slice x16, local copies, waits for them, and re-layouts, advance(): lax.dynamic_slice_in_dim(bra_shells, group_index * group_size, group_size...  12.1 us
    dot_general x1, matrix products, on_device(): lax.dot_general(ket_coeff, screened, (((0,), (1,)), ((), ())), preferred_...  10.2 us
  transfers between devices with their start and end apart: 2, of which 2 were waited for; matrix products, arithmetic and copies ran while one was open for 2% of the time, Pallas kernels for 0%

commit v1 on v0

v1 whole, which is shorter than its diff:
```python
import jax
import jax.numpy as jnp
from jax import lax
from jax.sharding import PartitionSpec as P

SHELL = 8
NI = 64
NA = 32


def shell_rows(mo_coeff, shells, start, count):
    table = mo_coeff.reshape(mo_coeff.shape[0] // SHELL, SHELL, mo_coeff.shape[1])
    rows = jnp.take(table, shells, axis=0)
    return lax.dynamic_slice_in_dim(rows, start, count, 2)


def on_device(ao_ints, shell_mask, bra_shells, ket_shells, mo_coeff, mo_ranges):
    local_bra = shell_mask.shape[0]
    local_ket = shell_mask.shape[1]
    pair_count = lax.axis_size("pair")
    batch_count = lax.axis_size("batch")
    place = lax.axis_index("pair")
    own_shells = lax.dynamic_slice_in_dim(bra_shells, place * local_bra, local_bra, 0)
    bra_one = shell_rows(mo_coeff, own_shells[:, 0], mo_ranges[2], NA)
    bra_two = shell_rows(mo_coeff, own_shells[:, 1], mo_ranges[3], NA)
    bra_coeff = (
        bra_one.astype(jnp.float32)[:, :, None, :, None] * bra_two.astype(jnp.float32)[:, None, :, None, :]
    ).reshape(local_bra * SHELL * SHELL, NA * NA).astype(jnp.bfloat16)
    block_mask = shell_mask.astype(jnp.bfloat16)
    screened = (
        ao_ints.reshape(local_bra, SHELL * SHELL, local_ket, SHELL * SHELL) * block_mask[:, None, :, None]
    ).reshape(ao_ints.shape)
    partial = lax.dot_general(
        bra_coeff, screened, (((0,), (0,)), ((), ())), preferred_element_type=jnp.float32
    )
    bra_done = lax.psum_scatter(partial, "pair", scatter_dimension=0, tiled=True)
    own_ab = bra_done.shape[0]
    ket_one = shell_rows(mo_coeff, ket_shells[:, 0], mo_ranges[0], NI)
    ket_two = shell_rows(mo_coeff, ket_shells[:, 1], mo_ranges[1], NI)
    ket_coeff = (
        ket_one.astype(jnp.float32)[:, :, None, :, None] * ket_two.astype(jnp.float32)[:, None, :, None, :]
    ).reshape(local_ket * SHELL * SHELL, NI * NI).astype(jnp.bfloat16)
    both = jnp.dot(bra_done.astype(jnp.bfloat16), ket_coeff, preferred_element_type=jnp.float32)
    split = both.reshape(own_ab, NI, batch_count, NI // batch_count)
    summed = lax.psum_scatter(split.transpose(2, 1, 3, 0), "batch", scatter_dimension=0, tiled=True)
    summed = summed.reshape(pair_count, NI // batch_count, own_ab)
    return lax.all_to_all(summed, "pair", split_axis=0, concat_axis=2, tiled=True).reshape(NI // batch_count, NA * NA)


def solution(mesh):
    return jax.shard_map(
        on_device,
        mesh=mesh,
        in_specs=(P("pair", "batch"), P("pair", "batch"), P(), P("batch", None), P(), P()),
        out_specs=P(("pair", "batch"), None),
        check_vma=False,
    )
```

time: 346 us -> 256 us (0.74)
  matrix products: 80.3 us -> 18.1 us
  other arithmetic: 57.3 us -> 10.4 us
  blocking collectives: 0 us -> 21.9 us
  loops' own time: 20 us -> 0 us
  waiting for transfers between devices: 102 us -> 122 us
  starting transfers between devices: 13.7 us -> 0.22 us
  local copies, waits for them, and re-layouts: 48.7 us -> 60.6 us
    reduce_scatter x1 -> x2, waiting for transfers between devices: 17.5 us -> 122 us  [the longest x1 95.8 us: on_device(): lax.psum_scatter(partial, 'pair', scatter_dimension=0, tiled=True)]
    all_to_all x1 -> x0, waiting for transfers between devices: 84.5 us -> none  [on_device(): lax.all_to_all(outgoing, 'pair', split_axis=0, concat_axis=2, tiled=True)]
    dot_general x85 -> x2, matrix products: 80.3 us -> 18.1 us  [the longest x1 13 us: on_device(): jnp.dot(bra_done.astype(jnp.bfloat16), ket_coeff, preferred_element_type=...]
    convert_element_type x17 -> x4, other arithmetic: 56.9 us -> 9.54 us  [the longest x1 6.54 us: on_device(): ket_coeff = (ket_one.astype(jnp.float32)[:, :, None, :, None] * ket_two.a...]
    convert_element_type x0 -> x2, local copies, waits for them, and re-layouts: none -> 29.7 us  [the longest x1 22.7 us: on_device(): ket_coeff = (ket_one.astype(jnp.float32)[:, :, None, :, None] * ket_two.a...]
    dynamic_slice x34 -> x1, local copies, waits for them, and re-layouts: 27.9 us -> 0.75 us  [on_device(): lax.dynamic_slice_in_dim(bra_shells, place * local_bra, local_bra, 0)]
    all_to_all x0 -> x1, blocking collectives: none -> 21.9 us  [on_device(): lax.all_to_all(summed, 'pair', split_axis=0, concat_axis=2, tiled=True)]
    another operation x1 -> x0, loops' own time: 20 us -> none  [bra_contract(): lax.scan(advance, starting, jnp.arange(shell_count // group_size, dtype=j...]
  transfers between devices with their start and end apart: 2 -> 2, of which waited for: 2 -> 2; matrix products, arithmetic and copies ran while one was open for 2% -> 17% of each run, Pallas kernels for 0% -> 0%
where the time goes in v1:
time: 256 us; the launch traced here: 254 us
  waiting for transfers between devices  122 us (48%)
  local copies, waits for them, and re-layouts  60.6 us (24%)
  blocking collectives  21.9 us (9%)
  between operations  20.9 us (8%)
  matrix products  18.1 us (7%)
  other arithmetic  10.4 us (4%)
    reduce_scatter x1, waiting for transfers between devices, on_device(): lax.psum_scatter(partial, 'pair', scatter_dimension=0, tiled=True)  95.8 us
    reduce_scatter x1, waiting for transfers between devices, on_device(): lax.psum_scatter(split.transpose(2, 1, 3, 0), 'batch', scatter_dimension=...  26.2 us
    convert_element_type x1, local copies, waits for them, and re-layouts, on_device(): ket_coeff = (ket_one.astype(jnp.float32)[:, :, None, :, None] * ket_two.a...  22.7 us
    all_to_all x1, blocking collectives, on_device(): lax.all_to_all(summed, 'pair', split_axis=0, concat_axis=2, tiled=True)  21.9 us
    dot_general x1, matrix products, on_device(): jnp.dot(bra_done.astype(jnp.bfloat16), ket_coeff, preferred_element_type=...  13 us
    dot_general x1, local copies, waits for them, and re-layouts, on_device(): jnp.dot(bra_done.astype(jnp.bfloat16), ket_coeff, preferred_element_type=...  12.1 us
    convert_element_type x1, local copies, waits for them, and re-layouts, on_device(): bra_coeff = (bra_one.astype(jnp.float32)[:, :, None, :, None] * bra_two.a...  7.01 us
    convert_element_type x1, other arithmetic, on_device(): ket_coeff = (ket_one.astype(jnp.float32)[:, :, None, :, None] * ket_two.a...  6.54 us
  transfers between devices with their start and end apart: 2, of which 2 were waited for; matrix products, arithmetic and copies ran while one was open for 17% of the time, Pallas kernels for 0%

profile of v1, /device:TPU:1, one launch (start us, length us, event | category | flops | bytes accessed | tf_op | source)
XLA Modules:
  0.0 254.2 jit_solution(2738407937939364442)
XLA Ops:
  6.5 0.0 copy-start
  6.5 0.0 copy-start.1
  6.5 0.0 reduce-scatter.3.cloned.1.call-start
  6.5 1.4 fusion.13
  10.4 0.8 constant_dynamic-slice_fusion
  11.2 0.0 copy-done
  11.2 0.6 gather_fusion
  11.8 0.6 gather_fusion.1
  13.5 0.1 fusion.11
  13.6 2.8 %multiply_convert_fusion.1 = bf16[8,8,8,32,32]{4,3,2,1,0:T(8,128)(2,1)} fusion(f32[8,8,32]{2,1,0:T(8,128)S(1)} %get-tuple-element.25, f32[8,8,32]{2,1,0:T(8,128)S(1)} %get-tuple-element.26), kind=kLoop, calls=%fused_computation.7 | loop fusion | flops 1048576 | bytes 1064960 | tf_op jit(solution)/shard_map/convert_element_type | solution.py:28
  16.4 7.0 %convert_element_type.33 = bf16[512,1024]{1,0:T(8,128)(2,1)} reshape(bf16[8,8,8,32,32]{4,3,2,1,0:T(8,128)(2,1)} %multiply_convert_fusion.1) | data formatting | bytes 2097152 | tf_op jit(solution)/shard_map/convert_element_type | solution.py:28
  23.4 0.0 copy-done.1
  23.4 1.7 mul.48
  25.1 0.0 copy-start.2
  25.1 4.1 %mul.49 = bf16[512,1024]{1,0:T(8,128)(2,1)} reshape(bf16[8,64,16,64]{3,2,1,0:T(8,128)(2,1)} %mul.48) | data formatting | bytes 2097152 | tf_op jit(solution)/shard_map/mul | solution.py:31
  29.2 5.1 %fusion.5 = f32[1024,1024]{1,0:T(8,128)} fusion(bf16[512,1024]{1,0:T(8,128)(2,1)} %convert_element_type.33, bf16[512,1024]{1,0:T(8,128)(2,1)} %param.10, bf16[512,1024]{1,0:T(8,128)(2,1)} %mul.49), kind=kOutput, calls=%fused_computation.9 | convolution fusion | flops 1074266112 | bytes 7340032 | tf_op jit(solution)/shard_map/dot_general | solution.py:33
  34.4 0.0 reduce-scatter.3.cloned.1.call-update
  34.4 0.2 reduce-scatter.5.cloned.1.call-start
  37.1 0.0 copy-done.2
  37.2 0.6 gather_fusion.2
  37.8 0.6 gather_fusion.3
  39.6 0.1 fusion.7
  39.7 6.5 %multiply_convert_fusion = bf16[16,8,8,64,64]{4,3,2,1,0:T(8,128)(2,1)} fusion(f32[16,8,64]{2,1,0:T(8,128)S(1)} %get-tuple-element.23, f32[16,8,64]{2,1,0:T(8,128)S(1)} %get-tuple-element.24), kind=kLoop, calls=%fused_computation.4 | loop fusion | flops 8388608 | bytes 8454144 | tf_op jit(solution)/shard_map/convert_element_type | solution.py:42
  46.2 22.7 %convert_element_type.39 = bf16[1024,4096]{1,0:T(8,128)(2,1)} reshape(bf16[16,8,8,64,64]{4,3,2,1,0:T(8,128)(2,1)} %multiply_convert_fusion) | data formatting | bytes 16777216 | tf_op jit(solution)/shard_map/convert_element_type | solution.py:42
  69.0 12.1 %copy.14 = bf16[4096,1024]{1,0:T(8,128)(2,1)} copy(bf16[4096,1024]{0,1:T(8,128)(2,1)} %bitcast.43) | data formatting | bytes 16777216 | tf_op jit(solution)/shard_map/dot_general | solution.py:43
  81.0 95.8 %reduce-scatter.3.cloned.1.call-done = f32[16,1024]{1,0:T(8,128)} async-done(((f32[1024,1024]{1,0:T(8,128)}), f32[16,1024]{1,0:T(8,128)}) %reduce-scatter.3.cloned.1.call-update) | async-done | bytes 65552 | tf_op jit(solution)/shard_map/reduce_scatter | solution.py:36
  176.8 13.0 %fusion.2 = f32[4,64,16,16]{1,3,2,0:T(8,128)} fusion(bf16[64,4,16,1024]{3,2,1,0:T(8,128)(2,1)} %bitcast.44, f32[16,1024]{1,0:T(8,128)} %reduce-scatter.3.cloned.1.call-done), kind=kOutput, calls=%fused_computation.8 | convolution fusion | flops 134234112 | bytes 8716288 | tf_op jit(solution)/shard_map/dot_general | solution.py:43
  189.8 0.0 reduce-scatter.5.cloned.1.call-update
  189.8 26.2 %reduce-scatter.5.cloned.1.call-done = f32[1,64,16,16]{1,3,2,0:T(8,128)} async-done(((f32[4,64,16,16]{1,3,2,0:T(8,128)}), f32[1,64,16,16]{1,3,2,0:T(8,128)}) %reduce-scatter.5.cloned.1.call-update) | async-done | bytes 65552 | tf_op jit(solution)/shard_map/reduce_scatter | solution.py:45
  216.0 1.9 copy.16
  217.9 1.3 reshape.91
  219.2 21.9 %all_to_all.15 = f32[64,1,256]{2,1,0:T(1,128)S(1)} all-to-all(f32[64,1,256]{2,1,0:T(1,128)S(1)} %reshape.91), channel_id=1, replica_groups=mesh['pair'=64,'batch'=4] {'pair'}, dimensions={0} | all-to-all | bytes 131072 | tf_op jit(solution)/shard_map/all_to_all | solution.py:47
  241.1 0.5 broadcast.94
  241.6 0.8 reduce
  242.4 1.0 reshape.92
  243.4 2.0 copy.17
  245.4 1.9 reshape.45
  (7 shorter events, 0.0 us)
Async XLA Ops:
  6.5 4.7 %copy-start = (bf16[6000,256]{1,0:T(8,128)(2,1)S(1)}, bf16[6000,256]{1,0:T(8,128)(2,1)}, u32[]{:S(2)}) copy-start(bf16[6000,256]{1,0:T(8,128)(2,1)} %param.14) | copy-start | bytes 9216004
  6.5 16.9 %copy-start.1 = (s32[8,16]{1,0:T(8,128)S(1)}, s32[8,16]{1,0:T(8,128)}, u32[]{:S(2)}) copy-start(s32[8,16]{1,0:T(8,128)} %param.11) | copy-start | bytes 1540
  6.5 170.2 %reduce-scatter.3.cloned.1.call-start = ((), (), s32[]{:S(2)}) async-start(), calls=%async_computation.3 | async-start | bytes 4259840 | tf_op jit(solution)/shard_map/reduce_scatter | solution.py:36
  25.1 12.0 %copy-start.2 = (s32[16,2]{0,1:T(2,128)S(1)}, s32[16,2]{0,1:T(2,128)}, u32[]{:S(2)}) copy-start(s32[16,2]{0,1:T(2,128)} %param.13) | copy-start | bytes 388
  34.4 181.6 %reduce-scatter.5.cloned.1.call-start = ((), (), s32[]{:S(2)}) async-start(), calls=%async_computation.4 | async-start | bytes 655360 | tf_op jit(solution)/shard_map/reduce_scatter | solution.py:45
Sparse Core Ops, SparseCore 0:
  34.5 142.2 reduce-scatter.2
  189.9 25.9 reduce-scatter.4

commit v2 on v1

v2 whole, which is shorter than its diff:
```python
import jax
import jax.numpy as jnp
from jax import lax
from jax.experimental import pallas as pl
from jax.experimental.pallas import tpu as pltpu
from jax.sharding import PartitionSpec as P

SHELL = 8
NX, NY, NZ, NC = 4, 4, 8, 2
OWN = 16
MESH = pl.DeviceIdType.MESH
BF = jnp.bfloat16
F32 = jnp.float32


def iota(shape, dim):
    return lax.broadcasted_iota(jnp.int32, shape, dim)


def where_one(condition):
    return jnp.where(condition, 1.0, 0.0).astype(BF)


def dot(a, b):
    return jnp.dot(a, b, preferred_element_type=F32)


def dot_last(a, b):
    return lax.dot_general(a, b, (((1,), (1,)), ((), ())), preferred_element_type=F32)


def pair_id(y, z, c):
    return (y * NZ + z) * NC + c


def kernel(
    ao_hbm, mask_ref, bra_ref, ket_ref, mo_hbm, ranges_ref, out_ref,
    ao_own, ao_other, mask_other, mo_table, bra_one, bra_two, ket_one, ket_two,
    bra_t, partial, to_y, from_y, to_z, from_z, own_sum, ket_wide, ket_narrow,
    spread, quarter, to_xy, from_xy, to_zc, from_zc,
    load_sem, core_send, core_recv, y_send, y_recv, z_send, z_recv, xy_send, xy_recv, zc_send, zc_recv,
):
    place = lax.axis_index("pair")
    x = lax.axis_index("batch")
    c = lax.rem(place, NC)
    z = lax.rem(place // NC, NZ)
    y = place // (NC * NZ)

    def plane_peer(dx, dy):
        return (pair_id(lax.rem(y + dy, NY), z, c), lax.rem(x + dx, NX))

    def line_peer(dz, dc):
        return (pair_id(y, lax.rem(z + dz, NZ), lax.rem(c + dc, NC)), x)

    load_ao = pltpu.make_async_copy(ao_hbm, ao_own, load_sem.at[0])
    load_mo = pltpu.make_async_copy(mo_hbm, mo_table, load_sem.at[1])
    load_mo.start()
    load_ao.start()
    barrier = pltpu.get_barrier_semaphore()
    plane = [(dx, dy) for dx in range(NX) for dy in range(NY) if dx or dy]
    line = [(dz, dc) for dz in range(NZ) for dc in range(NC) if dz or dc]
    for dx, dy in plane:
        pl.semaphore_signal(barrier, inc=1, device_id=plane_peer(dx, dy), device_id_type=MESH)
    for dz, dc in line:
        pl.semaphore_signal(barrier, inc=1, device_id=line_peer(dz, dc), device_id_type=MESH)

    load_mo.wait()
    half = mask_ref.shape[0]
    first_pair = place * half
    other_pair = pair_id(y, z, lax.rem(c + 1, NC)) * half

    def take_bra(t, carry):
        spot = pl.ds(pl.multiple_of(t * SHELL, SHELL), SHELL)
        late = pl.ds(pl.multiple_of((half + t) * SHELL, SHELL), SHELL)
        bra_one[spot, :] = mo_table[bra_ref[first_pair + t, 0]].astype(F32)
        bra_two[spot, :] = mo_table[bra_ref[first_pair + t, 1]].astype(F32)
        bra_one[late, :] = mo_table[bra_ref[other_pair + t, 0]].astype(F32)
        bra_two[late, :] = mo_table[bra_ref[other_pair + t, 1]].astype(F32)
        return carry

    lax.fori_loop(0, half, take_bra, 0)

    def take_ket(s, carry):
        spot = pl.ds(pl.multiple_of(s * SHELL, SHELL), SHELL)
        ket_one[spot, :] = mo_table[ket_ref[s, 0]].astype(F32)
        ket_two[spot, :] = mo_table[ket_ref[s, 1]].astype(F32)
        return carry

    lax.fori_loop(0, ket_ref.shape[0], take_ket, 0)

    depth = bra_one.shape[0]
    width = bra_t.shape[1]
    orbitals = bra_one.shape[1]
    row = iota((bra_t.shape[0], orbitals), 0)
    piece = row >> 7
    to_z_place = (z + jnp.where(((row >> 4) & 1) == 0, 4 + piece, 3 - piece)) & (NZ - 1)
    to_y_place = (y + ((row >> 5) & 3)) & (NY - 1)
    ab = to_z_place * 128 + c * 64 + to_y_place * 16 + (row & 15)
    orbital = iota((bra_t.shape[0], orbitals), 1)
    pick_a = where_one(orbital == ranges_ref[2] + (ab >> 5))
    pick_b = where_one(orbital == ranges_ref[3] + (ab & 31))
    small_a = dot_last(pick_a, bra_one[...].astype(BF)).astype(BF)
    small_b = dot_last(pick_b, bra_two[...].astype(BF)).astype(BF)
    source = iota((depth, width), 0)
    column = iota((depth, width), 1)
    over_m = where_one(source == (column >> 3))
    over_n = where_one(((source >> 3) == (column >> 6)) & ((source & 7) == (column & 7)))
    for start in range(0, bra_t.shape[0], 128):
        rows = slice(start, start + 128)
        bra_t[rows, :] = (dot(small_a[rows], over_m) * dot(small_b[rows], over_n)).astype(BF)

    mask_spread = where_one(
        iota((mask_ref.shape[1], ao_own.shape[1]), 0) == (iota((mask_ref.shape[1], ao_own.shape[1]), 1) >> 6)
    )

    def screen(values, mask):
        wide = dot(mask[...].astype(F32).astype(BF), mask_spread).astype(BF)
        for t in range(half):
            block = slice(64 * t, 64 * t + 64)
            values[block, :] = values[block, :] * wide[t:t + 1, :]

    pl.semaphore_wait(barrier, len(plane) + len(line))

    ao_copy = pltpu.make_async_remote_copy(
        ao_hbm, ao_other, core_send.at[0], core_recv.at[0], device_id=line_peer(0, 1), device_id_type=MESH
    )
    mask_copy = pltpu.make_async_remote_copy(
        mask_ref, mask_other, core_send.at[1], core_recv.at[1], device_id=line_peer(0, 1), device_id_type=MESH
    )
    mask_copy.start()
    ao_copy.start()

    load_ao.wait()
    screen(ao_own, mask_ref)
    own_width = ao_own.shape[0]

    def own_part(p, carry):
        rows = pl.ds(pl.multiple_of(p * 128, 128), 128)
        partial[rows, :] = dot(bra_t[rows, :own_width], ao_own[...])
        return carry

    lax.fori_loop(0, 4, own_part, 0)
    mask_copy.wait_recv()
    ao_copy.wait_recv()
    screen(ao_other, mask_other)

    def y_copy(p, dy):
        return pltpu.make_async_remote_copy(
            to_y.at[p, dy - 1], from_y.at[p, dy - 1], y_send.at[p, dy - 1], y_recv.at[p, dy - 1],
            device_id=plane_peer(0, dy), device_id_type=MESH,
        )

    def other_part(p, carry):
        rows = pl.ds(pl.multiple_of(p * 128, 128), 128)
        total = partial[rows, :] + dot(bra_t[rows, own_width:], ao_other[...])
        own_sum[p] = total[:32]
        for dy in (2, 1, 3):
            to_y[p, dy - 1] = total[32 * dy:32 * dy + 32].astype(BF)
            y_copy(p, dy).start()
        return carry

    lax.fori_loop(0, 4, other_part, 0)

    columns = spread.shape[1]
    col = iota((orbitals, columns), 1)
    first = (((y + (col >> 8)) & (NY - 1)) << 4) + (((z + ((col >> 5) & 7)) & (NZ - 1)) << 1) + ((c + (col >> 4)) & 1)
    pick_i = where_one(iota((orbitals, columns), 0) == ranges_ref[0] + first)
    spread[...] = dot(ket_one[...].astype(BF), pick_i)
    j_row = iota((ket_narrow.shape[0], orbitals), 0)
    second = (((x + (j_row >> 4)) & (NX - 1)) << 4) + (j_row & 15)
    pick_j = where_one(iota((ket_narrow.shape[0], orbitals), 1) == ranges_ref[1] + second)
    narrow = dot_last(pick_j, ket_two[...].astype(BF)).astype(BF)
    ket_narrow[...] = jnp.concatenate([narrow, narrow], axis=1)

    def z_copy(dz):
        return pltpu.make_async_remote_copy(
            to_z.at[dz - 1], from_z.at[dz - 1], z_send.at[dz - 1], z_recv.at[dz - 1],
            device_id=line_peer(dz, 0), device_id_type=MESH,
        )

    summed = None
    for p in range(4):
        for dy in range(1, NY):
            y_copy(p, dy).wait_recv()
        total = own_sum[p] + from_y[p, 0].astype(F32) + from_y[p, 1].astype(F32) + from_y[p, 2].astype(F32)
        for part, dz in ((total[:16], 4 + p), (total[16:], 3 - p)):
            if dz == 0:
                summed = part
            else:
                to_z[dz - 1] = part.astype(BF)
                z_copy(dz).start()
    for dz in (1, 7, 2, 6, 3, 5, 4):
        z_copy(dz).wait_recv()
        summed = summed + from_z[dz - 1].astype(F32)

    high = summed.astype(BF)
    low = (summed - high.astype(F32)).astype(BF)
    lanes = where_one((iota((2 * OWN, 128), 0) & 15) == (iota((2 * OWN, 128), 1) & 15))
    ket_wide[...] = lax.dot_general(
        jnp.concatenate([high, low], axis=0), lanes, (((0,), (0,)), ((), ())), preferred_element_type=F32
    )

    def over_first(s, carry):
        sums = [None] * (columns // 128)
        factors = spread[pl.ds(pl.multiple_of(s * SHELL, SHELL), SHELL), :]
        for m in range(SHELL):
            block = ket_wide[pl.ds(pl.multiple_of((s * SHELL + m) * SHELL, SHELL), SHELL), :]
            for tile in range(columns // 128):
                term = factors[m:m + 1, 128 * tile:128 * tile + 128] * block
                sums[tile] = term if m == 0 else sums[tile] + term
        for tile in range(columns // 128):
            quarter[pl.ds(pl.multiple_of(s * SHELL, SHELL), SHELL), 128 * tile:128 * tile + 128] = sums[tile]
        return carry

    lax.fori_loop(0, spread.shape[0] // SHELL, over_first, 0)
    value = quarter[...]
    value_high = value.astype(BF)
    value_low = (value - value_high.astype(F32)).astype(BF)
    both = dot(ket_narrow[...], jnp.concatenate([value_high, value_low], axis=0))

    def plane_copy(dx, dy, slot):
        return pltpu.make_async_remote_copy(
            to_xy.at[dx, dy], from_xy.at[slot[0], slot[1]], xy_send.at[dx * NY + dy], xy_recv.at[dx * NY + dy],
            device_id=plane_peer(dx, dy), device_id_type=MESH,
        )

    for dx, dy in sorted(plane, key=lambda d: -min(d[0], NX - d[0]) - min(d[1], NY - d[1])):
        to_xy[dx, dy] = both[16 * dx:16 * dx + 16, 256 * dy:256 * dy + 256]
        plane_copy(dx, dy, (y, x)).start()
    from_xy[y, x] = both[:16, :256]
    for dx, dy in plane:
        plane_copy(dx, dy, (lax.rem(y + NY - dy, NY), lax.rem(x + NX - dx, NX))).wait_recv()
    merged = [from_xy[k, 0] + from_xy[k, 1] + from_xy[k, 2] + from_xy[k, 3] for k in range(NY)]

    def line_copy(dz, dc, slot):
        return pltpu.make_async_remote_copy(
            to_zc.at[dz * NC + dc], from_zc.at[slot[0], slot[1]], zc_send.at[dz * NC + dc], zc_recv.at[dz * NC + dc],
            device_id=line_peer(dz, dc), device_id_type=MESH,
        )

    lane = iota((8, 128), 1)
    for dz, dc in sorted([(dz, dc) for dz in range(NZ) for dc in range(NC)], key=lambda d: -min(d[0], NZ - d[0])):
        group = dz * NC + dc
        tile = slice(128 * (group // 8), 128 * (group // 8) + 128)
        message = None
        for k in range(8):
            block = merged[k % 4][8 * (k // 4):8 * (k // 4) + 8, tile]
            shift = (16 * k - 16 * (group % 8)) % 128
            moved = pltpu.roll(block, shift, 1) if shift else block
            message = moved if message is None else jnp.where((lane >> 4) == k, moved, message)
        if group:
            to_zc[group] = message
            line_copy(dz, dc, (z, c)).start()
        else:
            from_zc[z, c] = message
    for dz, dc in line:
        line_copy(dz, dc, (lax.rem(z + NZ - dz, NZ), lax.rem(c + NC - dc, NC))).wait_recv()
    for k in range(NZ):
        left, right = from_zc[k, 0], from_zc[k, 1]
        out_ref[0:8, 128 * k:128 * k + 128] = jnp.where(lane < 64, left, pltpu.roll(right, 64, 1))
        out_ref[8:16, 128 * k:128 * k + 128] = jnp.where(lane < 64, pltpu.roll(left, 64, 1), right)

    mask_copy.wait_send()
    ao_copy.wait_send()
    for p in range(4):
        for dy in range(1, NY):
            y_copy(p, dy).wait_send()
    for dz in range(1, NZ):
        z_copy(dz).wait_send()
    for dx, dy in plane:
        plane_copy(dx, dy, (y, x)).wait_send()
    for dz, dc in line:
        line_copy(dz, dc, (z, c)).wait_send()


def on_device(ao_ints, shell_mask, bra_shells, ket_shells, mo_coeff, mo_ranges):
    table = mo_coeff.reshape(mo_coeff.shape[0] // SHELL, SHELL, mo_coeff.shape[1])
    rows, cols = ao_ints.shape
    orbitals = mo_coeff.shape[1]
    ket_rows = ket_shells.shape[0] * SHELL
    bra_rows = NC * shell_mask.shape[0] * SHELL
    dma = pltpu.SemaphoreType.DMA
    whole = pl.BlockSpec(memory_space=pl.ANY)
    scalar = pl.BlockSpec(memory_space=pltpu.SMEM)
    vector = pl.BlockSpec(memory_space=pltpu.VMEM)
    return pl.pallas_call(
        kernel,
        out_shape=jax.ShapeDtypeStruct((16, 1024), F32),
        in_specs=[whole, vector, scalar, scalar, whole, scalar],
        out_specs=vector,
        scratch_shapes=[
            pltpu.VMEM((rows, cols), BF),
            pltpu.VMEM((rows, cols), BF),
            pltpu.VMEM(shell_mask.shape, jnp.int32),
            pltpu.VMEM(table.shape, BF),
            pltpu.VMEM((bra_rows, orbitals), F32),
            pltpu.VMEM((bra_rows, orbitals), F32),
            pltpu.VMEM((ket_rows, orbitals), F32),
            pltpu.VMEM((ket_rows, orbitals), F32),
            pltpu.VMEM((512, NC * rows), BF),
            pltpu.VMEM((512, cols), F32),
            pltpu.VMEM((4, NY - 1, 32, cols), BF),
            pltpu.VMEM((4, NY - 1, 32, cols), BF),
            pltpu.VMEM((NZ - 1, OWN, cols), BF),
            pltpu.VMEM((NZ - 1, OWN, cols), BF),
            pltpu.VMEM((4, 32, cols), F32),
            pltpu.VMEM((cols, 128), F32),
            pltpu.VMEM((64, 2 * ket_rows), BF),
            pltpu.VMEM((ket_rows, 1024), F32),
            pltpu.VMEM((ket_rows, 1024), F32),
            pltpu.VMEM((NX, NY, 16, 256), F32),
            pltpu.VMEM((NY, NX, 16, 256), F32),
            pltpu.VMEM((NZ * NC, 8, 128), F32),
            pltpu.VMEM((NZ, NC, 8, 128), F32),
            dma((2,)),
            dma((2,)),
            dma((2,)),
            dma((4, NY - 1)),
            dma((4, NY - 1)),
            dma((NZ - 1,)),
            dma((NZ - 1,)),
            dma((NX * NY,)),
            dma((NX * NY,)),
            dma((NZ * NC,)),
            dma((NZ * NC,)),
        ],
        compiler_params=pltpu.CompilerParams(collective_id=0, has_side_effects=True, vmem_limit_bytes=40 * 1024 * 1024),
    )(ao_ints, shell_mask, bra_shells, ket_shells, table, mo_ranges)


def solution(mesh):
    return jax.shard_map(
        on_device,
        mesh=mesh,
        in_specs=(P("pair", "batch"), P("pair", "batch"), P(), P("batch", None), P(), P()),
        out_specs=P(("pair", "batch"), None),
        check_vma=False,
    )
```

time: 256 us -> 54.4 us (0.21)
  waiting for transfers between devices: 122 us -> 0 us
  local copies, waits for them, and re-layouts: 60.6 us -> 6.64 us
  Pallas kernels: 0 us -> 47.5 us
  blocking collectives: 21.9 us -> 0 us
  between operations: 20.9 us -> 0.03 us
  matrix products: 18.1 us -> 0 us
  other arithmetic: 10.4 us -> 0 us
    reduce_scatter x2 -> x0, waiting for transfers between devices: 122 us -> none  [the longest x1 95.8 us: on_device(): lax.psum_scatter(partial, 'pair', scatter_dimension=0, tiled=True)]
    pallas_call x0 -> x1, Pallas kernels: none -> 47.5 us  [on_device(): pl.pallas_call(kernel, out_shape=jax.ShapeDtypeStruct((16, 1024), F32), i...]
    convert_element_type x2 -> x0, local copies, waits for them, and re-layouts: 29.7 us -> none  [the longest x1 22.7 us: on_device(): ket_coeff = (ket_one.astype(jnp.float32)[:, :, None, :, None] * ket_two.a...]
    all_to_all x1 -> x0, blocking collectives: 21.9 us -> none  [on_device(): lax.all_to_all(summed, 'pair', split_axis=0, concat_axis=2, tiled=True)]
    dot_general x2 -> x0, matrix products: 18.1 us -> none  [the longest x1 13 us: on_device(): jnp.dot(bra_done.astype(jnp.bfloat16), ket_coeff, preferred_element_type=...]
    dot_general x1 -> x0, local copies, waits for them, and re-layouts: 12.1 us -> none  [on_device(): jnp.dot(bra_done.astype(jnp.bfloat16), ket_coeff, preferred_element_type=...]
    convert_element_type x5 -> x0, other arithmetic: 9.55 us -> none  [the longest x1 6.54 us: on_device(): ket_coeff = (ket_one.astype(jnp.float32)[:, :, None, :, None] * ket_two.a...]
    mul x2 -> x0, local copies, waits for them, and re-layouts: 5.8 us -> none  [on_device(): ao_ints.reshape(local_bra, SHELL * SHELL, local_ket, SHELL * SHELL)]
  transfers between devices with their start and end apart: 2 -> 0, of which waited for: 2 -> 0; matrix products, arithmetic and copies ran while one was open for 17% -> 0% of each run, Pallas kernels for 0% -> 0%
where the time goes in v2:
time: 54.4 us; the launch traced here: 54.2 us
  Pallas kernels  47.5 us (87%)
  local copies, waits for them, and re-layouts  6.64 us (12%)
    pallas_call x1, Pallas kernels, on_device(): pl.pallas_call(kernel, out_shape=jax.ShapeDtypeStruct((16, 1024), F32), i...  47.5 us
    unnamed x11, local copies, waits for them, and re-layouts  6.64 us

profile of v2, /device:TPU:1, one launch (start us, length us, event | category | flops | bytes accessed | tf_op | source)
XLA Modules:
  0.0 54.2 jit_solution(7298524504606824604)
XLA Ops:
  0.0 0.8 %copy.8.ket_ref = s32[16,2]{1,0:T(8,128)S(1)} copy(s32[16,2]{0,1:T(2,128)} %param.9) | data formatting | bytes 256 | tf_op args[3]
  0.8 0.8 %copy.7.bra_ref = s32[512,2]{1,0:T(8,128)S(1)} copy(s32[512,2]{0,1:T(2,128)} %param.8) | data formatting | bytes 8192 | tf_op args[2]
  1.6 0.0 copy-start
  1.6 1.9 %copy-done = bf16[6000,256]{1,0:T(8,128)(2,1)S(1)} copy-done((bf16[6000,256]{1,0:T(8,128)(2,1)S(1)}, bf16[6000,256]{1,0:T(8,128)(2,1)}, u32[]{:S(2)}) %copy-start) | copy-done | bytes 3072024
  3.5 0.0 copy-start.1
  3.5 1.2 %copy-done.1 = bf16[512,1024]{1,0:T(8,128)(2,1)S(1)} copy-done((bf16[512,1024]{1,0:T(8,128)(2,1)S(1)}, bf16[512,1024]{1,0:T(8,128)(2,1)}, u32[]{:S(2)}) %copy-start.1) | copy-done | bytes 1048600
  4.7 0.0 copy-start.2
  4.7 0.7 %copy-done.2 = s32[8,16]{1,0:T(8,128)S(1)} copy-done((s32[8,16]{1,0:T(8,128)S(1)}, s32[8,16]{1,0:T(8,128)}, u32[]{:S(2)}) %copy-start.2) | copy-done | bytes 536
  5.4 0.0 copy-start.3
  5.4 0.7 %copy-done.3 = s32[4]{0:T(128)S(1)} copy-done((s32[4]{0:T(128)S(1)}, s32[4]{0:T(128)}, u32[]{:S(2)}) %copy-start.3) | copy-done | bytes 40
  6.0 47.5 %shard_map.64 = f32[16,1024]{1,0:T(8,128)S(1)} custom-call(bf16[512,1024]{1,0:T(8,128)(2,1)S(1)} %copy-done.1, s32[8,16]{1,0:T(8,128)S(1)} %copy-done.2, s32[512,2]{1,0:T(8,128)S(1)} %copy.7.bra_ref, s32[16,2]{1,0:T(8,128)S(1)} %copy.8.ket_ref, bf16[750,8,256]{2,1,0:T(8,128)(2,1)S(1)} %bitcast.1, s32[4]{0:T(128)S(1)} %copy-done.3), custom_call_target="tpu_custom_call" | custom-call | tf_op jit(solution)/shard_map/pallas_call | solution.py:286
  53.6 0.6 %copy.10 = f32[16,1024]{1,0:T(8,128)} copy(f32[16,1024]{1,0:T(8,128)S(1)} %shard_map.64) | data formatting | bytes 131072
Async XLA Ops:
  1.6 1.9 %copy-start = (bf16[6000,256]{1,0:T(8,128)(2,1)S(1)}, bf16[6000,256]{1,0:T(8,128)(2,1)}, u32[]{:S(2)}) copy-start(bf16[6000,256]{1,0:T(8,128)(2,1)} %param.10) | copy-start | bytes 9216004
  3.5 1.2 %copy-start.1 = (bf16[512,1024]{1,0:T(8,128)(2,1)S(1)}, bf16[512,1024]{1,0:T(8,128)(2,1)}, u32[]{:S(2)}) copy-start(bf16[512,1024]{1,0:T(8,128)(2,1)} %ao_hbm.1) | copy-start | bytes 3145732
  4.7 0.7 %copy-start.2 = (s32[8,16]{1,0:T(8,128)S(1)}, s32[8,16]{1,0:T(8,128)}, u32[]{:S(2)}) copy-start(s32[8,16]{1,0:T(8,128)} %mask_ref.1) | copy-start | bytes 1540
  5.4 0.7 %copy-start.3 = (s32[4]{0:T(128)S(1)}, s32[4]{0:T(128)}, u32[]{:S(2)}) copy-start(s32[4]{0:T(128)} %ranges_ref.1) | copy-start | bytes 52

commit v3 on v2

--- a/solution.py
+++ b/solution.py
@@ -8,6 +8,8 @@
 SHELL = 8
 NX, NY, NZ, NC = 4, 4, 8, 2
 OWN = 16
+PARTS, PART = 4, 256
+LAG = 2
 MESH = pl.DeviceIdType.MESH
 BF = jnp.bfloat16
 F32 = jnp.float32
@@ -37,7 +39,7 @@
     ao_hbm, mask_ref, bra_ref, ket_ref, mo_hbm, ranges_ref, out_ref,
     ao_own, ao_other, mask_other, mo_table, bra_one, bra_two, ket_one, ket_two,
     bra_t, partial, to_y, from_y, to_z, from_z, own_sum, ket_wide, ket_narrow,
-    spread, quarter, to_xy, from_xy, to_zc, from_zc,
+    wide_other, own_z, spread, quarter, to_xy, from_xy, to_zc, from_zc,
     load_sem, core_send, core_recv, y_send, y_recv, z_send, z_recv, xy_send, xy_recv, zc_send, zc_recv,
 ):
     place = lax.axis_index("pair")
@@ -52,10 +54,16 @@
     def line_peer(dz, dc):
         return (pair_id(y, lax.rem(z + dz, NZ), lax.rem(c + dc, NC)), x)
 
-    load_ao = pltpu.make_async_copy(ao_hbm, ao_own, load_sem.at[0])
-    load_mo = pltpu.make_async_copy(mo_hbm, mo_table, load_sem.at[1])
+    def part_of(p):
+        return pl.ds(pl.multiple_of(p * PART, PART), PART)
+
+    def load_ao(p):
+        return pltpu.make_async_copy(ao_hbm.at[:, part_of(p)], ao_own.at[:, part_of(p)], load_sem.at[p])
+
+    load_mo = pltpu.make_async_copy(mo_hbm, mo_table, load_sem.at[PARTS])
     load_mo.start()
-    load_ao.start()
+    for p in range(PARTS):
+        load_ao(p).start()
     barrier = pltpu.get_barrier_semaphore()
     plane = [(dx, dy) for dx in range(NX) for dy in range(NY) if dx or dy]
     line = [(dz, dc) for dz in range(NZ) for dc in range(NC) if dz or dc]
@@ -72,29 +80,43 @@
     def take_bra(t, carry):
         spot = pl.ds(pl.multiple_of(t * SHELL, SHELL), SHELL)
         late = pl.ds(pl.multiple_of((half + t) * SHELL, SHELL), SHELL)
-        bra_one[spot, :] = mo_table[bra_ref[first_pair + t, 0]].astype(F32)
-        bra_two[spot, :] = mo_table[bra_ref[first_pair + t, 1]].astype(F32)
-        bra_one[late, :] = mo_table[bra_ref[other_pair + t, 0]].astype(F32)
-        bra_two[late, :] = mo_table[bra_ref[other_pair + t, 1]].astype(F32)
+        bra_one[spot, :] = mo_table[bra_ref[0, first_pair + t]].astype(F32)
+        bra_two[spot, :] = mo_table[bra_ref[1, first_pair + t]].astype(F32)
+        bra_one[late, :] = mo_table[bra_ref[0, other_pair + t]].astype(F32)
+        bra_two[late, :] = mo_table[bra_ref[1, other_pair + t]].astype(F32)
         return carry
 
     lax.fori_loop(0, half, take_bra, 0)
 
     def take_ket(s, carry):
         spot = pl.ds(pl.multiple_of(s * SHELL, SHELL), SHELL)
-        ket_one[spot, :] = mo_table[ket_ref[s, 0]].astype(F32)
-        ket_two[spot, :] = mo_table[ket_ref[s, 1]].astype(F32)
-        return carry
-
-    lax.fori_loop(0, ket_ref.shape[0], take_ket, 0)
+        ket_one[spot, :] = mo_table[ket_ref[0, s]].astype(F32)
+        ket_two[spot, :] = mo_table[ket_ref[1, s]].astype(F32)
+        return carry
+
+    lax.fori_loop(0, ket_ref.shape[1], take_ket, 0)
+
+    pl.semaphore_wait(barrier, len(plane) + len(line))
+
+    def ao_copy(p):
+        return pltpu.make_async_remote_copy(
+            ao_hbm.at[:, part_of(p)], ao_other.at[:, part_of(p)], core_send.at[p], core_recv.at[p],
+            device_id=line_peer(0, 1), device_id_type=MESH,
+        )
+
+    mask_copy = pltpu.make_async_remote_copy(
+        mask_ref, mask_other, core_send.at[PARTS], core_recv.at[PARTS], device_id=line_peer(0, 1), device_id_type=MESH
+    )
+    mask_copy.start()
+    for p in range(PARTS):
+        ao_copy(p).start()
 
     depth = bra_one.shape[0]
     width = bra_t.shape[1]
     orbitals = bra_one.shape[1]
     row = iota((bra_t.shape[0], orbitals), 0)
-    piece = row >> 7
-    to_z_place = (z + jnp.where(((row >> 4) & 1) == 0, 4 + piece, 3 - piece)) & (NZ - 1)
-    to_y_place = (y + ((row >> 5) & 3)) & (NY - 1)
+    to_z_place = (z + ((row >> 4) & 7)) & (NZ - 1)
+    to_y_place = (y + (row >> 7)) & (NY - 1)
     ab = to_z_place * 128 + c * 64 + to_y_place * 16 + (row & 15)
     orbital = iota((bra_t.shape[0], orbitals), 1)
     pick_a = where_one(orbital == ranges_ref[2] + (ab >> 5))
@@ -113,36 +135,28 @@
         iota((mask_ref.shape[1], ao_own.shape[1]), 0) == (iota((mask_ref.shape[1], ao_own.shape[1]), 1) >> 6)
     )
 
-    def screen(values, mask):
-        wide = dot(mask[...].astype(F32).astype(BF), mask_spread).astype(BF)
+    own_wide = dot(mask_ref[...].astype(F32).astype(BF), mask_spread)
+    wide_other[0] = own_wide
+
+    def screen(values, wide, p):
+        factor = wide[:, part_of(p)].astype(BF)
         for t in range(half):
             block = slice(64 * t, 64 * t + 64)
-            values[block, :] = values[block, :] * wide[t:t + 1, :]
-
-    pl.semaphore_wait(barrier, len(plane) + len(line))
-
-    ao_copy = pltpu.make_async_remote_copy(
-        ao_hbm, ao_other, core_send.at[0], core_recv.at[0], device_id=line_peer(0, 1), device_id_type=MESH
-    )
-    mask_copy = pltpu.make_async_remote_copy(
-        mask_ref, mask_other, core_send.at[1], core_recv.at[1], device_id=line_peer(0, 1), device_id_type=MESH
-    )
-    mask_copy.start()
-    ao_copy.start()
-
-    load_ao.wait()
-    screen(ao_own, mask_ref)
+            values[block, part_of(p)] = values[block, part_of(p)] * factor[t:t + 1, :]
+
     own_width = ao_own.shape[0]
 
     def own_part(p, carry):
-        rows = pl.ds(pl.multiple_of(p * 128, 128), 128)
-        partial[rows, :] = dot(bra_t[rows, :own_width], ao_own[...])
-        return carry
-
-    lax.fori_loop(0, 4, own_part, 0)
+        load_ao(p).wait()
+        screen(ao_own, wide_other.at[0], p)
+        for dy in range(NY):
+            rows = slice(128 * dy, 128 * dy + 128)
+            partial[rows, part_of(p)] = dot(bra_t[rows, :own_width], ao_own[:, part_of(p)])
+        return carry
+
+    lax.fori_loop(0, PARTS, own_part, 0)
     mask_copy.wait_recv()
-    ao_copy.wait_recv()
-    screen(ao_other, mask_other)
+    wide_other[1] = dot(mask_other[...].astype(F32).astype(BF), mask_spread)
 
     def y_copy(p, dy):
         return pltpu.make_async_remote_copy(
@@ -151,15 +165,19 @@
         )
 
     def other_part(p, carry):
-        rows = pl.ds(pl.multiple_of(p * 128, 128), 128)
-        total = partial[rows, :] + dot(bra_t[rows, own_width:], ao_other[...])
-        own_sum[p] = total[:32]
-        for dy in (2, 1, 3):
-            to_y[p, dy - 1] = total[32 * dy:32 * dy + 32].astype(BF)
-            y_copy(p, dy).start()
-        return carry
-
-    lax.fori_loop(0, 4, other_part, 0)
+        ao_copy(p).wait_recv()
+        screen(ao_other, wide_other.at[1], p)
+        for dy in (2, 1, 3, 0):
+            rows = slice(128 * dy, 128 * dy + 128)
+            total = partial[rows, part_of(p)] + dot(bra_t[rows, own_width:], ao_other[:, part_of(p)])
+            if dy:
+                to_y[p, dy - 1] = total.astype(BF)
+                y_copy(p, dy).start()
+            else:
+                own_sum[p] = total
+        return carry
+
+    lax.fori_loop(0, PARTS, other_part, 0)
 
     columns = spread.shape[1]
     col = iota((orbitals, columns), 1)
@@ -172,33 +190,27 @@
     narrow = dot_last(pick_j, ket_two[...].astype(BF)).astype(BF)
     ket_narrow[...] = jnp.concatenate([narrow, narrow], axis=1)
 
-    def z_copy(dz):
-        return pltpu.make_async_remote_copy(
-            to_z.at[dz - 1], from_z.at[dz - 1], z_send.at[dz - 1], z_recv.at[dz - 1],
+    def z_copy(p, dz):
+        return pltpu.make_async_remote_copy(
+            to_z.at[p, dz - 1], from_z.at[p, dz - 1], z_send.at[p, dz - 1], z_recv.at[p, dz - 1],
             device_id=line_peer(dz, 0), device_id_type=MESH,
         )
 
-    summed = None
-    for p in range(4):
+    def over_y(p):
         for dy in range(1, NY):
             y_copy(p, dy).wait_recv()
-        total = own_sum[p] + from_y[p, 0].astype(F32) + from_y[p, 1].astype(F32) + from_y[p, 2].astype(F32)
-        for part, dz in ((total[:16], 4 + p), (total[16:], 3 - p)):
-            if dz == 0:
-                summed = part
+        for dz in (4, 3, 5, 2, 6, 1, 7, 0):
+            rows = slice(OWN * dz, OWN * dz + OWN)
+            part = own_sum[p, rows]
+            for dy in range(1, NY):
+                part = part + from_y[p, dy - 1, rows].astype(F32)
+            if dz:
+                to_z[p, dz - 1] = part.astype(BF)
+                z_copy(p, dz).start()
             else:
-                to_z[dz - 1] = part.astype(BF)
-                z_copy(dz).start()
-    for dz in (1, 7, 2, 6, 3, 5, 4):
-        z_copy(dz).wait_recv()
-        summed = summed + from_z[dz - 1].astype(F32)
-
-    high = summed.astype(BF)
-    low = (summed - high.astype(F32)).astype(BF)
+                own_z[p] = part
+
     lanes = where_one((iota((2 * OWN, 128), 0) & 15) == (iota((2 * OWN, 128), 1) & 15))
-    ket_wide[...] = lax.dot_general(
-        jnp.concatenate([high, low], axis=0), lanes, (((0,), (0,)), ((), ())), preferred_element_type=F32
-    )
 
     def over_first(s, carry):
         sums = [None] * (columns // 128)
@@ -212,7 +224,36 @@
             quarter[pl.ds(pl.multiple_of(s * SHELL, SHELL), SHELL), 128 * tile:128 * tile + 128] = sums[tile]
         return carry
 
-    lax.fori_loop(0, spread.shape[0] // SHELL, over_first, 0)
+    pairs = PART // (SHELL * SHELL)
+
+    def over_z(p):
+        summed = own_z[p]
+        for dz in (1, 7, 2, 6, 3, 5, 4):
+            z_copy(p, dz).wait_recv()
+            summed = summed + from_z[p, dz - 1].astype(F32)
+        high = summed.astype(BF)
+        low = (summed - high.astype(F32)).astype(BF)
+        ket_wide[part_of(p), :] = lax.dot_general(
+            jnp.concatenate([high, low], axis=0), lanes, (((0,), (0,)), ((), ())), preferred_element_type=F32
+        )
+        lax.fori_loop(p * pairs, p * pairs + pairs, over_first, 0)
+
+    def step(p, carry):
+        over_y(p)
+        return carry
+
+    def both_steps(p, carry):
+        over_y(p)
+        over_z(p - LAG)
+        return carry
+
+    def last_step(p, carry):
+        over_z(p)
+        return carry
+
+    lax.fori_loop(0, LAG, step, 0)
+    lax.fori_loop(LAG, PARTS, both_steps, 0)
+    lax.fori_loop(PARTS - LAG, PARTS, last_step, 0)
     value = quarter[...]
     value_high = value.astype(BF)
     value_low = (value - value_high.astype(F32)).astype(BF)
@@ -261,12 +302,16 @@
         out_ref[8:16, 128 * k:128 * k + 128] = jnp.where(lane < 64, pltpu.roll(left, 64, 1), right)
 
     mask_copy.wait_send()
-    ao_copy.wait_send()
-    for p in range(4):
+
+    def drain(p, carry):
+        ao_copy(p).wait_send()
         for dy in range(1, NY):
             y_copy(p, dy).wait_send()
-    for dz in range(1, NZ):
-        z_copy(dz).wait_send()
+        for dz in range(1, NZ):
+            z_copy(p, dz).wait_send()
+        return carry
+
+    lax.fori_loop(0, PARTS, drain, 0)
     for dx, dy in plane:
         plane_copy(dx, dy, (y, x)).wait_send()
     for dz, dc in line:
@@ -280,7 +325,7 @@
     ket_rows = ket_shells.shape[0] * SHELL
     bra_rows = NC * shell_mask.shape[0] * SHELL
     dma = pltpu.SemaphoreType.DMA
-    whole = pl.BlockSpec(memory_space=pl.ANY)
+    whole = pl.BlockSpec(memory_space=pltpu.HBM)
     scalar = pl.BlockSpec(memory_space=pltpu.SMEM)
     vector = pl.BlockSpec(memory_space=pltpu.VMEM)
     return pl.pallas_call(
@@ -299,33 +344,35 @@
             pltpu.VMEM((ket_rows, orbitals), F32),
             pltpu.VMEM((512, NC * rows), BF),
             pltpu.VMEM((512, cols), F32),
-            pltpu.VMEM((4, NY - 1, 32, cols), BF),
-            pltpu.VMEM((4, NY - 1, 32, cols), BF),
-            pltpu.VMEM((NZ - 1, OWN, cols), BF),
-            pltpu.VMEM((NZ - 1, OWN, cols), BF),
-            pltpu.VMEM((4, 32, cols), F32),
+            pltpu.VMEM((PARTS, NY - 1, NZ * OWN, PART), BF),
+            pltpu.VMEM((PARTS, NY - 1, NZ * OWN, PART), BF),
+            pltpu.VMEM((PARTS, NZ - 1, OWN, PART), BF),
+            pltpu.VMEM((PARTS, NZ - 1, OWN, PART), BF),
+            pltpu.VMEM((PARTS, NZ * OWN, PART), F32),
             pltpu.VMEM((cols, 128), F32),
             pltpu.VMEM((64, 2 * ket_rows), BF),
+            pltpu.VMEM((NC, shell_mask.shape[0], cols), F32),
+            pltpu.VMEM((PARTS, OWN, PART), F32),
             pltpu.VMEM((ket_rows, 1024), F32),
             pltpu.VMEM((ket_rows, 1024), F32),
             pltpu.VMEM((NX, NY, 16, 256), F32),
             pltpu.VMEM((NY, NX, 16, 256), F32),
             pltpu.VMEM((NZ * NC, 8, 128), F32),
             pltpu.VMEM((NZ, NC, 8, 128), F32),
-            dma((2,)),
-            dma((2,)),
-            dma((2,)),
-            dma((4, NY - 1)),
-            dma((4, NY - 1)),
-            dma((NZ - 1,)),
-            dma((NZ - 1,)),
+            dma((PARTS + 1,)),
+            dma((PARTS + 1,)),
+            dma((PARTS + 1,)),
+            dma((PARTS, NY - 1)),
+            dma((PARTS, NY - 1)),
+            dma((PARTS, NZ - 1)),
+            dma((PARTS, NZ - 1)),
             dma((NX * NY,)),
             dma((NX * NY,)),
             dma((NZ * NC,)),
             dma((NZ * NC,)),
         ],
-        compiler_params=pltpu.CompilerParams(collective_id=0, has_side_effects=True, vmem_limit_bytes=40 * 1024 * 1024),
-    )(ao_ints, shell_mask, bra_shells, ket_shells, table, mo_ranges)
+        compiler_params=pltpu.CompilerParams(collective_id=0, has_side_effects=True, vmem_limit_bytes=67_043_328),
+    )(ao_ints, shell_mask, bra_shells.T, ket_shells.T, table, mo_ranges)
 
 
 def solution(mesh):

time: 54.4 us -> 47.2 us (0.87)
  local copies, waits for them, and re-layouts: 6.64 us -> 1.47 us
  Pallas kernels: 47.5 us -> 45.6 us
    unnamed x11 -> x1, local copies, waits for them, and re-layouts: 6.64 us -> 1.47 us
    pallas_call x1, Pallas kernels: 47.5 us -> 45.6 us  [on_device(): pl.pallas_call(kernel, out_shape=jax.ShapeDtypeStruct((16, 1024), F32), i...]
where the time goes in v3:
time: 47.2 us; the launch traced here: 47.1 us
  Pallas kernels  45.6 us (97%)
  local copies, waits for them, and re-layouts  1.47 us (3%)
    pallas_call x1, Pallas kernels, on_device(): pl.pallas_call(kernel, out_shape=jax.ShapeDtypeStruct((16, 1024), F32), i...  45.6 us
    unnamed x1, local copies, waits for them, and re-layouts  1.47 us

profile of v3, /device:TPU:1, one launch (start us, length us, event | category | flops | bytes accessed | tf_op | source)
XLA Modules:
  0.0 47.1 jit_solution(1353548086608517517)
XLA Ops:
  0.0 45.6 %shard_map.64 = f32[16,1024]{1,0:T(8,128)} custom-call(bf16[512,1024]{1,0:T(8,128)(2,1)} %ao_hbm.1, s32[8,16]{1,0:T(8,128)} %mask_ref.1, s32[2,512]{1,0:T(2,128)} %bitcast.4, s32[2,16]{1,0:T(2,128)} %bitcast.5, bf16[750,8,256]{2,1,0:T(8,128)(2,1)} %bitcast.3, s32[4]{0:T(128)} %ranges_ref.1), custom_call_target="tpu_custom_call" | custom-call | tf_op jit(solution)/shard_map/pallas_call | solution.py:331
  45.6 1.5 %copy.8 = f32[16,1024]{1,0:T(8,128)} copy(f32[16,1024]{1,0:T(8,128)} %shard_map.64) | data formatting | bytes 131072

commit v4 on v3

--- a/solution.py
+++ b/solution.py
@@ -39,8 +39,8 @@
     ao_hbm, mask_ref, bra_ref, ket_ref, mo_hbm, ranges_ref, out_ref,
     ao_own, ao_other, mask_other, mo_table, bra_one, bra_two, ket_one, ket_two,
     bra_t, partial, to_y, from_y, to_z, from_z, own_sum, ket_wide, ket_narrow,
-    wide_other, own_z, spread, quarter, to_xy, from_xy, to_zc, from_zc,
-    load_sem, core_send, core_recv, y_send, y_recv, z_send, z_recv, xy_send, xy_recv, zc_send, zc_recv,
+    wide_other, own_z, to_relay, from_relay, kept, spread, quarter, to_xy, from_xy, to_zc, from_zc,
+    load_sem, core_send, core_recv, y_send, y_recv, relay_send, relay_recv, z_send, z_recv, xy_send, xy_recv, zc_send, zc_recv,
 ):
     place = lax.axis_index("pair")
     x = lax.axis_index("batch")
@@ -158,26 +158,53 @@
     mask_copy.wait_recv()
     wide_other[1] = dot(mask_other[...].astype(F32).astype(BF), mask_spread)
 
-    def y_copy(p, dy):
-        return pltpu.make_async_remote_copy(
-            to_y.at[p, dy - 1], from_y.at[p, dy - 1], y_send.at[p, dy - 1], y_recv.at[p, dy - 1],
-            device_id=plane_peer(0, dy), device_id_type=MESH,
+    ways = (1, NY - 1)
+    rows_y = NZ * OWN
+    half_rows = (slice(0, rows_y // 2), slice(rows_y // 2, rows_y))
+
+    def y_copy(p, way, part):
+        return pltpu.make_async_remote_copy(
+            to_y.at[p, way, part], from_y.at[p, way, part], y_send.at[p, way, part], y_recv.at[p, way, part],
+            device_id=plane_peer(0, ways[way]), device_id_type=MESH,
+        )
+
+    def relay_copy(p, way):
+        return pltpu.make_async_remote_copy(
+            to_relay.at[p, way], from_relay.at[p, way], relay_send.at[p, way], relay_recv.at[p, way],
+            device_id=plane_peer(0, ways[way]), device_id_type=MESH,
         )
 
     def other_part(p, carry):
         ao_copy(p).wait_recv()
         screen(ao_other, wide_other.at[1], p)
         for dy in (2, 1, 3, 0):
-            rows = slice(128 * dy, 128 * dy + 128)
+            rows = slice(rows_y * dy, rows_y * dy + rows_y)
             total = partial[rows, part_of(p)] + dot(bra_t[rows, own_width:], ao_other[:, part_of(p)])
-            if dy:
-                to_y[p, dy - 1] = total.astype(BF)
-                y_copy(p, dy).start()
+            if dy == 0:
+                own_sum[p] = total
+            elif dy == 2:
+                for way in range(2):
+                    to_relay[p, way] = total[half_rows[way]].astype(BF)
+                    relay_copy(p, way).start()
             else:
-                own_sum[p] = total
-        return carry
-
-    lax.fori_loop(0, PARTS, other_part, 0)
+                way = ways.index(dy)
+                kept[p, way] = total[half_rows[way]]
+                to_y[p, way, 1 - way] = total[half_rows[1 - way]].astype(BF)
+                y_copy(p, way, 1 - way).start()
+        return carry
+
+    def relay(p, carry):
+        for way in range(2):
+            relay_copy(p, way).wait_recv()
+            to_y[p, way, way] = (kept[p, way] + from_relay[p, way].astype(F32)).astype(BF)
+            y_copy(p, way, way).start()
+        return carry
+
+    def other_and_relay(p, carry):
+        return relay(p - LAG, other_part(p, carry))
+
+    lax.fori_loop(0, LAG, other_part, 0)
+    lax.fori_loop(LAG, PARTS, other_and_relay, 0)
 
     columns = spread.shape[1]
     col = iota((orbitals, columns), 1)
@@ -197,13 +224,14 @@
         )
 
     def over_y(p):
-        for dy in range(1, NY):
-            y_copy(p, dy).wait_recv()
+        for way in range(2):
+            for part in (1 - way, way):
+                y_copy(p, way, part).wait_recv()
         for dz in (4, 3, 5, 2, 6, 1, 7, 0):
-            rows = slice(OWN * dz, OWN * dz + OWN)
-            part = own_sum[p, rows]
-            for dy in range(1, NY):
-                part = part + from_y[p, dy - 1, rows].astype(F32)
+            part = own_sum[p, OWN * dz:OWN * dz + OWN]
+            start = OWN * dz % (rows_y // 2)
+            for way in range(2):
+                part = part + from_y[p, way, 2 * dz // NZ, start:start + OWN].astype(F32)
             if dz:
                 to_z[p, dz - 1] = part.astype(BF)
                 z_copy(p, dz).start()
@@ -239,6 +267,7 @@
         lax.fori_loop(p * pairs, p * pairs + pairs, over_first, 0)
 
     def step(p, carry):
+        relay(p + PARTS - LAG, 0)
         over_y(p)
         return carry
 
@@ -305,8 +334,10 @@
 
     def drain(p, carry):
         ao_copy(p).wait_send()
-        for dy in range(1, NY):
-            y_copy(p, dy).wait_send()
+        for way in range(2):
+            relay_copy(p, way).wait_send()
+            y_copy(p, way, 0).wait_send()
+            y_copy(p, way, 1).wait_send()
         for dz in range(1, NZ):
             z_copy(p, dz).wait_send()
         return carry
@@ -344,8 +375,8 @@
             pltpu.VMEM((ket_rows, orbitals), F32),
             pltpu.VMEM((512, NC * rows), BF),
             pltpu.VMEM((512, cols), F32),
-            pltpu.VMEM((PARTS, NY - 1, NZ * OWN, PART), BF),
-            pltpu.VMEM((PARTS, NY - 1, NZ * OWN, PART), BF),
+            pltpu.VMEM((PARTS, 2, 2, NZ * OWN // 2, PART), BF),
+            pltpu.VMEM((PARTS, 2, 2, NZ * OWN // 2, PART), BF),
             pltpu.VMEM((PARTS, NZ - 1, OWN, PART), BF),
             pltpu.VMEM((PARTS, NZ - 1, OWN, PART), BF),
             pltpu.VMEM((PARTS, NZ * OWN, PART), F32),
@@ -353,6 +384,9 @@
             pltpu.VMEM((64, 2 * ket_rows), BF),
             pltpu.VMEM((NC, shell_mask.shape[0], cols), F32),
             pltpu.VMEM((PARTS, OWN, PART), F32),
+            pltpu.VMEM((PARTS, 2, NZ * OWN // 2, PART), BF),
+            pltpu.VMEM((PARTS, 2, NZ * OWN // 2, PART), BF),
+            pltpu.VMEM((PARTS, 2, NZ * OWN // 2, PART), F32),
             pltpu.VMEM((ket_rows, 1024), F32),
             pltpu.VMEM((ket_rows, 1024), F32),
             pltpu.VMEM((NX, NY, 16, 256), F32),
@@ -362,8 +396,10 @@
             dma((PARTS + 1,)),
             dma((PARTS + 1,)),
             dma((PARTS + 1,)),
-            dma((PARTS, NY - 1)),
-            dma((PARTS, NY - 1)),
+            dma((PARTS, 2, 2)),
+            dma((PARTS, 2, 2)),
+            dma((PARTS, 2)),
+            dma((PARTS, 2)),
             dma((PARTS, NZ - 1)),
             dma((PARTS, NZ - 1)),
             dma((NX * NY,)),

time: 47.2 us -> 46.3 us (0.981)
  Pallas kernels: 45.6 us -> 44.6 us
    pallas_call x1, Pallas kernels: 45.6 us -> 44.6 us  [on_device(): pl.pallas_call(kernel, out_shape=jax.ShapeDtypeStruct((16, 1024), F32), i...]
where the time goes in v4:
time: 46.3 us; the launch traced here: 46.1 us
  Pallas kernels  44.6 us (96%)
  local copies, waits for them, and re-layouts  1.47 us (3%)
    pallas_call x1, Pallas kernels, on_device(): pl.pallas_call(kernel, out_shape=jax.ShapeDtypeStruct((16, 1024), F32), i...  44.6 us
    unnamed x1, local copies, waits for them, and re-layouts  1.47 us

profile of v4, /device:TPU:1, one launch (start us, length us, event | category | flops | bytes accessed | tf_op | source)
XLA Modules:
  0.0 46.1 jit_solution(11907530026894833885)
XLA Ops:
  0.0 44.6 %shard_map.64 = f32[16,1024]{1,0:T(8,128)} custom-call(bf16[512,1024]{1,0:T(8,128)(2,1)} %ao_hbm.1, s32[8,16]{1,0:T(8,128)} %mask_ref.1, s32[2,512]{1,0:T(2,128)} %bitcast.4, s32[2,16]{1,0:T(2,128)} %bitcast.5, bf16[750,8,256]{2,1,0:T(8,128)(2,1)} %bitcast.3, s32[4]{0:T(128)} %ranges_ref.1), custom_call_target="tpu_custom_call" | custom-call | tf_op jit(solution)/shard_map/pallas_call | solution.py:362
  44.6 1.5 %copy.8 = f32[16,1024]{1,0:T(8,128)} copy(f32[16,1024]{1,0:T(8,128)} %shard_map.64) | data formatting | bytes 131072

commit v5 on v4

--- a/solution.py
+++ b/solution.py
@@ -95,21 +95,6 @@
         return carry
 
     lax.fori_loop(0, ket_ref.shape[1], take_ket, 0)
-
-    pl.semaphore_wait(barrier, len(plane) + len(line))
-
-    def ao_copy(p):
-        return pltpu.make_async_remote_copy(
-            ao_hbm.at[:, part_of(p)], ao_other.at[:, part_of(p)], core_send.at[p], core_recv.at[p],
-            device_id=line_peer(0, 1), device_id_type=MESH,
-        )
-
-    mask_copy = pltpu.make_async_remote_copy(
-        mask_ref, mask_other, core_send.at[PARTS], core_recv.at[PARTS], device_id=line_peer(0, 1), device_id_type=MESH
-    )
-    mask_copy.start()
-    for p in range(PARTS):
-        ao_copy(p).start()
 
     depth = bra_one.shape[0]
     width = bra_t.shape[1]
@@ -131,6 +116,21 @@
         rows = slice(start, start + 128)
         bra_t[rows, :] = (dot(small_a[rows], over_m) * dot(small_b[rows], over_n)).astype(BF)
 
+    pl.semaphore_wait(barrier, len(plane) + len(line))
+
+    def ao_copy(p):
+        return pltpu.make_async_remote_copy(
+            ao_hbm.at[:, part_of(p)], ao_other.at[:, part_of(p)], core_send.at[p], core_recv.at[p],
+            device_id=line_peer(0, 1), device_id_type=MESH,
+        )
+
+    mask_copy = pltpu.make_async_remote_copy(
+        mask_ref, mask_other, core_send.at[PARTS], core_recv.at[PARTS], device_id=line_peer(0, 1), device_id_type=MESH
+    )
+    mask_copy.start()
+    for p in range(PARTS):
+        ao_copy(p).start()
+
     mask_spread = where_one(
         iota((mask_ref.shape[1], ao_own.shape[1]), 0) == (iota((mask_ref.shape[1], ao_own.shape[1]), 1) >> 6)
     )
@@ -267,22 +267,22 @@
         lax.fori_loop(p * pairs, p * pairs + pairs, over_first, 0)
 
     def step(p, carry):
-        relay(p + PARTS - LAG, 0)
         over_y(p)
         return carry
 
     def both_steps(p, carry):
         over_y(p)
-        over_z(p - LAG)
+        over_z(p - 3)
         return carry
 
     def last_step(p, carry):
         over_z(p)
         return carry
 
-    lax.fori_loop(0, LAG, step, 0)
-    lax.fori_loop(LAG, PARTS, both_steps, 0)
-    lax.fori_loop(PARTS - LAG, PARTS, last_step, 0)
+    lax.fori_loop(PARTS - LAG, PARTS, relay, 0)
+    lax.fori_loop(0, 3, step, 0)
+    lax.fori_loop(3, PARTS, both_steps, 0)
+    lax.fori_loop(PARTS - 3, PARTS, last_step, 0)
     value = quarter[...]
     value_high = value.astype(BF)
     value_low = (value - value_high.astype(F32)).astype(BF)
@@ -295,12 +295,12 @@
         )
 
     for dx, dy in sorted(plane, key=lambda d: -min(d[0], NX - d[0]) - min(d[1], NY - d[1])):
-        to_xy[dx, dy] = both[16 * dx:16 * dx + 16, 256 * dy:256 * dy + 256]
+        to_xy[dx, dy] = both[16 * dx:16 * dx + 16, 256 * dy:256 * dy + 256].astype(BF)
         plane_copy(dx, dy, (y, x)).start()
-    from_xy[y, x] = both[:16, :256]
+    from_xy[y, x] = both[:16, :256].astype(BF)
     for dx, dy in plane:
         plane_copy(dx, dy, (lax.rem(y + NY - dy, NY), lax.rem(x + NX - dx, NX))).wait_recv()
-    merged = [from_xy[k, 0] + from_xy[k, 1] + from_xy[k, 2] + from_xy[k, 3] for k in range(NY)]
+    merged = [from_xy[k, 0].astype(F32) + from_xy[k, 1].astype(F32) + from_xy[k, 2].astype(F32) + from_xy[k, 3].astype(F32) for k in range(NY)]
 
     def line_copy(dz, dc, slot):
         return pltpu.make_async_remote_copy(
@@ -389,8 +389,8 @@
             pltpu.VMEM((PARTS, 2, NZ * OWN // 2, PART), F32),
             pltpu.VMEM((ket_rows, 1024), F32),
             pltpu.VMEM((ket_rows, 1024), F32),
-            pltpu.VMEM((NX, NY, 16, 256), F32),
-            pltpu.VMEM((NY, NX, 16, 256), F32),
+            pltpu.VMEM((NX, NY, 16, 256), BF),
+            pltpu.VMEM((NY, NX, 16, 256), BF),
             pltpu.VMEM((NZ * NC, 8, 128), F32),
             pltpu.VMEM((NZ, NC, 8, 128), F32),
             dma((PARTS + 1,)),

time: 46.3 us -> 44.8 us (0.968)
  Pallas kernels: 44.6 us -> 43.1 us
    pallas_call x1, Pallas kernels: 44.6 us -> 43.1 us  [on_device(): pl.pallas_call(kernel, out_shape=jax.ShapeDtypeStruct((16, 1024), F32), i...]
where the time goes in v5:
time: 44.8 us; the launch traced here: 44.6 us
  Pallas kernels  43.1 us (96%)
  local copies, waits for them, and re-layouts  1.47 us (3%)
    pallas_call x1, Pallas kernels, on_device(): pl.pallas_call(kernel, out_shape=jax.ShapeDtypeStruct((16, 1024), F32), i...  43.1 us
    unnamed x1, local copies, waits for them, and re-layouts  1.47 us

profile of v5, /device:TPU:1, one launch (start us, length us, event | category | flops | bytes accessed | tf_op | source)
XLA Modules:
  0.0 44.6 jit_solution(11251353751906361575)
XLA Ops:
  0.0 43.1 %shard_map.64 = f32[16,1024]{1,0:T(8,128)} custom-call(bf16[512,1024]{1,0:T(8,128)(2,1)} %ao_hbm.1, s32[8,16]{1,0:T(8,128)} %mask_ref.1, s32[2,512]{1,0:T(2,128)} %bitcast.4, s32[2,16]{1,0:T(2,128)} %bitcast.5, bf16[750,8,256]{2,1,0:T(8,128)(2,1)} %bitcast.3, s32[4]{0:T(128)} %ranges_ref.1), custom_call_target="tpu_custom_call" | custom-call | tf_op jit(solution)/shard_map/pallas_call | solution.py:362
  43.1 1.5 %copy.8 = f32[16,1024]{1,0:T(8,128)} copy(f32[16,1024]{1,0:T(8,128)} %shard_map.64) | data formatting | bytes 131072

commit v6 on v5

--- a/solution.py
+++ b/solution.py
@@ -155,6 +155,18 @@
         return carry
 
     lax.fori_loop(0, PARTS, own_part, 0)
+
+    columns = spread.shape[1]
+    col = iota((orbitals, columns), 1)
+    first = (((y + (col >> 8)) & (NY - 1)) << 4) + (((z + ((col >> 5) & 7)) & (NZ - 1)) << 1) + ((c + (col >> 4)) & 1)
+    pick_i = where_one(iota((orbitals, columns), 0) == ranges_ref[0] + first)
+    spread[...] = dot(ket_one[...].astype(BF), pick_i)
+    j_row = iota((ket_narrow.shape[0], orbitals), 0)
+    second = (((x + (j_row >> 4)) & (NX - 1)) << 4) + (j_row & 15)
+    pick_j = where_one(iota((ket_narrow.shape[0], orbitals), 1) == ranges_ref[1] + second)
+    narrow = dot_last(pick_j, ket_two[...].astype(BF)).astype(BF)
+    ket_narrow[...] = jnp.concatenate([narrow, narrow], axis=1)
+
     mask_copy.wait_recv()
     wide_other[1] = dot(mask_other[...].astype(F32).astype(BF), mask_spread)
 
@@ -205,17 +217,6 @@
 
     lax.fori_loop(0, LAG, other_part, 0)
     lax.fori_loop(LAG, PARTS, other_and_relay, 0)
-
-    columns = spread.shape[1]
-    col = iota((orbitals, columns), 1)
-    first = (((y + (col >> 8)) & (NY - 1)) << 4) + (((z + ((col >> 5) & 7)) & (NZ - 1)) << 1) + ((c + (col >> 4)) & 1)
-    pick_i = where_one(iota((orbitals, columns), 0) == ranges_ref[0] + first)
-    spread[...] = dot(ket_one[...].astype(BF), pick_i)
-    j_row = iota((ket_narrow.shape[0], orbitals), 0)
-    second = (((x + (j_row >> 4)) & (NX - 1)) << 4) + (j_row & 15)
-    pick_j = where_one(iota((ket_narrow.shape[0], orbitals), 1) == ranges_ref[1] + second)
-    narrow = dot_last(pick_j, ket_two[...].astype(BF)).astype(BF)
-    ket_narrow[...] = jnp.concatenate([narrow, narrow], axis=1)
 
     def z_copy(p, dz):
         return pltpu.make_async_remote_copy(

time: 44.8 us -> 45 us (level)
  no operation moved by 1% of the time
where the time goes in v6:
time: 45 us; the launch traced here: 44.8 us
  Pallas kernels  43.4 us (96%)
  local copies, waits for them, and re-layouts  1.47 us (3%)
    pallas_call x1, Pallas kernels, on_device(): pl.pallas_call(kernel, out_shape=jax.ShapeDtypeStruct((16, 1024), F32), i...  43.4 us
    unnamed x1, local copies, waits for them, and re-layouts  1.47 us

profile of v6, /device:TPU:1, one launch (start us, length us, event | category | flops | bytes accessed | tf_op | source)
XLA Modules:
  0.0 44.8 jit_solution(9662659945355501304)
XLA Ops:
  0.0 43.4 %shard_map.64 = f32[16,1024]{1,0:T(8,128)} custom-call(bf16[512,1024]{1,0:T(8,128)(2,1)} %ao_hbm.1, s32[8,16]{1,0:T(8,128)} %mask_ref.1, s32[2,512]{1,0:T(2,128)} %bitcast.4, s32[2,16]{1,0:T(2,128)} %bitcast.5, bf16[750,8,256]{2,1,0:T(8,128)(2,1)} %bitcast.3, s32[4]{0:T(128)} %ranges_ref.1), custom_call_target="tpu_custom_call" | custom-call | tf_op jit(solution)/shard_map/pallas_call | solution.py:363
  43.4 1.5 %copy.8 = f32[16,1024]{1,0:T(8,128)} copy(f32[16,1024]{1,0:T(8,128)} %shard_map.64) | data formatting | bytes 131072
